TPU v7x, 128 devices: a whole 4x4x4 slice. The times are simulated.
128 devices in a mesh: dp: 64 (over z, y, x), tensor: 2 (over core).
Axes of the slice: x: 4, y: 4, z: 4, core: 2. Of those that a mesh axis runs over, the one named last changes fastest.
Arguments:
- tokens: bfloat16 [49152, 768], P(('dp', 'tensor')), may hold values from -6 to 6
- skip_tokens: bfloat16 [49152, 768], P(('dp', 'tensor')), may hold values from -6 to 6
- cot_back: bfloat16 [49152, 768], P(('dp', 'tensor')), may hold values from -6 to 6
- cot_head: bfloat16 [49152, 768], P(('dp', 'tensor')), may hold values from -6 to 6
- one_span: int32 [192], P('dp'), may hold values 0 or 1
- lower_qkv: bfloat16 [3, 768, 768], P(None, None, 'tensor'), may hold values from -0.21875 to 0.21875
- lower_proj: bfloat16 [768, 768], P('tensor'), may hold values from -1.75 to 1.75
- lower_gain_attn: float32 [768], replicated, may hold values from 0.1 to 1.9
- lower_shift_attn: float32 [768], replicated, may hold values from -1.5 to 1.5
- lower_w_in: bfloat16 [768, 3072], P(None, 'tensor'), may hold values from -0.21875 to 0.21875
- lower_w_out: bfloat16 [3072, 768], P('tensor'), may hold values from -0.15625 to 0.15625
- lower_gain_ffn: float32 [768], replicated, may hold values from 0.1 to 1.9
- lower_shift_ffn: float32 [768], replicated, may hold values from -1.5 to 1.5
- upper_qkv: bfloat16 [3, 768, 768], P(None, None, 'tensor'), may hold values from -0.21875 to 0.21875
- upper_proj: bfloat16 [768, 768], P('tensor'), may hold values from -1.75 to 1.75
- upper_gain_attn: float32 [768], replicated, may hold values from 0.1 to 1.9
- upper_shift_attn: float32 [768], replicated, may hold values from -1.5 to 1.5
- upper_w_in: bfloat16 [768, 3072], P(None, 'tensor'), may hold values from -0.21875 to 0.21875
- upper_w_out: bfloat16 [3072, 768], P('tensor'), may hold values from -0.15625 to 0.15625
- upper_gain_ffn: float32 [768], replicated, may hold values from 0.1 to 1.9
- upper_shift_ffn: float32 [768], replicated, may hold values from -1.5 to 1.5
Outputs:
- back_out: bfloat16 [49152, 768], P(('dp', 'tensor'))
- head_out: bfloat16 [49152, 768], P(('dp', 'tensor'))
- grad_tokens: float32 [49152, 768], P(('dp', 'tensor'))
- grad_skip: float32 [49152, 768], P(('dp', 'tensor'))
- grad_lower_qkv: float32 [3, 768, 768], P(None, None, 'tensor')
- grad_lower_proj: float32 [768, 768], P('tensor')
- grad_lower_gain_attn: float32 [768], replicated
- grad_lower_shift_attn: float32 [768], replicated
- grad_lower_w_in: float32 [768, 3072], P(None, 'tensor')
- grad_lower_w_out: float32 [3072, 768], P('tensor')
- grad_lower_gain_ffn: float32 [768], replicated
- grad_lower_shift_ffn: float32 [768], replicated
- grad_upper_qkv: float32 [3, 768, 768], P(None, None, 'tensor')
- grad_upper_proj: float32 [768, 768], P('tensor')
- grad_upper_gain_attn: float32 [768], replicated
- grad_upper_shift_attn: float32 [768], replicated
- grad_upper_w_in: float32 [768, 3072], P(None, 'tensor')
- grad_upper_w_out: float32 [3072, 768], P('tensor')
- grad_upper_gain_ffn: float32 [768], replicated
- grad_upper_shift_ffn: float32 [768], replicated
Inputs may be any that keep to these rules, and one draw needn't show every extreme that they name: `one_span`: 1 marks a document whose second span is padding: masked as keys, and zero in both outputs.
All inputs are finite; a program needn't handle non-finite values. No bound on the sum of `one_span` on one device may be relied on, other than what follows from the above.
Results may differ from a plain program's by a relative error of at most 0.02.
Values may be sent and summed in bfloat16 or wider, within the bound.
No kernel may reach another device: no remote copies, remote signals or barrier semaphores. Data moves between devices by JAX's collectives and lax.ppermute only.
A program may use at most 192 MiB of HBM per device.

v0:
```python
import jax
import jax.numpy as jnp
from jax import lax
from jax.sharding import PartitionSpec as P

HEAD_DIM = 64
SPAN = 128
EPS = 1e-06
SCALE = 0.125
NEG = -1000000000.0


def norm_forward(resid, gain, shift):
    mean = jnp.mean(resid, axis=-1, keepdims=True)
    centered = resid - mean
    var = jnp.mean(centered * centered, axis=-1, keepdims=True)
    inv_std = lax.rsqrt(var + EPS)
    normed = centered * inv_std
    return (normed * gain + shift, normed, inv_std)


def norm_backward(grad_out, normed, inv_std, gain):
    grad_normed = grad_out * gain
    first_mean = jnp.mean(grad_normed, axis=-1, keepdims=True)
    second_mean = jnp.mean(grad_normed * normed, axis=-1, keepdims=True)
    grad_resid = inv_std * (grad_normed - first_mean - normed * second_mean)
    return (grad_resid, jnp.sum(grad_out * normed, axis=0), jnp.sum(grad_out, axis=0))


def gelu_slope(value):
    return (
        0.5 * (1.0 + jax.scipy.special.erf(value * 0.7071067811865476))
        + value * jnp.exp(-0.5 * value * value) * 0.3989422804014327
    )


def contract_last(left, right):
    return lax.dot_general(
        left, right, (((1,), (1,)), ((), ())), preferred_element_type=jnp.float32
    )


def contract_rows(left, right):
    return lax.dot_general(
        left, right, (((0,), (0,)), ((), ())), preferred_element_type=jnp.float32
    )


def gather_rows(rows_low):
    return lax.all_gather(rows_low, "tensor", axis=0, tiled=True)


def gather_grad(rows_low):
    return lax.all_gather(rows_low, "tensor", axis=0, tiled=True)


def sum_rows(full, weight, count):

    def term(start, size):
        return jnp.dot(full, weight, preferred_element_type=jnp.float32)

    return lax.psum_scatter(
        term(jnp.int32(0), count * lax.axis_size("tensor")).astype(jnp.bfloat16),
        "tensor",
        scatter_dimension=0,
        tiled=True,
    ).astype(jnp.float32)


def sum_back(term, count):
    return lax.psum_scatter(
        term(jnp.int32(0), count * lax.axis_size("tensor")).astype(jnp.bfloat16),
        "tensor",
        scatter_dimension=0,
        tiled=True,
    ).astype(jnp.float32)


def split_heads(full_qkv, index, docs):
    rows, _, width = full_qkv.shape
    return full_qkv[:, index].reshape(docs, 2 * SPAN, width // HEAD_DIM, HEAD_DIM)


def attend(qkv, key_ok):
    docs = key_ok.shape[0]
    rows, _, width = qkv.shape
    query = split_heads(qkv, 0, docs).astype(jnp.bfloat16)
    keys = split_heads(qkv, 1, docs).astype(jnp.bfloat16)
    values = split_heads(qkv, 2, docs).astype(jnp.bfloat16)
    scores = jnp.einsum("nqhe,nkhe->nhqk", query, keys, preferred_element_type=jnp.float32) * SCALE
    scores = jnp.where(key_ok[:, None, None, :], scores, NEG)
    largest = jnp.max(scores, axis=-1, keepdims=True)
    raised = jnp.exp(scores - largest)
    total = jnp.sum(raised, axis=-1, keepdims=True)
    log_total = largest + jnp.log(total)
    prob_low = (raised / total).astype(jnp.bfloat16)
    mixed = jnp.einsum("nhqk,nkhe->nqhe", prob_low, values, preferred_element_type=jnp.float32)
    context = mixed.reshape(rows, width).astype(jnp.bfloat16)
    return (context, (query, keys, values, log_total))


def attend_back(grad_ctx, kept, key_ok):
    query, keys, values, log_total = kept
    docs, length, heads, size = query.shape
    scores = jnp.einsum("nqhe,nkhe->nhqk", query, keys, preferred_element_type=jnp.float32) * SCALE
    scores = jnp.where(key_ok[:, None, None, :], scores, NEG)
    prob = jnp.exp(scores - log_total)
    prob_low = prob.astype(jnp.bfloat16)
    grad_mix = grad_ctx.reshape(docs, length, heads, size)
    grad_values = jnp.einsum(
        "nhqk,nqhe->nkhe", prob_low, grad_mix, preferred_element_type=jnp.float32
    )
    grad_prob = jnp.einsum("nqhe,nkhe->nhqk", grad_mix, values, preferred_element_type=jnp.float32)
    grad_scores = prob * (grad_prob - jnp.sum(grad_prob * prob, axis=-1, keepdims=True))
    grad_scores = grad_scores.astype(jnp.bfloat16)
    grad_query = (
        jnp.einsum("nhqk,nkhe->nqhe", grad_scores, keys, preferred_element_type=jnp.float32) * SCALE
    )
    grad_keys = (
        jnp.einsum("nhqk,nqhe->nkhe", grad_scores, query, preferred_element_type=jnp.float32)
        * SCALE
    )
    rows = docs * length
    width = heads * size
    stacked = jnp.stack(
        [
            grad_query.reshape(rows, width),
            grad_keys.reshape(rows, width),
            grad_values.reshape(rows, width),
        ],
        axis=1,
    )
    return stacked.astype(jnp.bfloat16)


def block_forward(rows, weights, key_ok, count):
    qkv_w, proj_w, gain_a, shift_a, in_w, out_w, gain_f, shift_f = weights
    full = gather_rows(rows.astype(jnp.bfloat16))
    qkv = jnp.einsum("rd,cdj->rcj", full, qkv_w, preferred_element_type=jnp.float32)
    context, att_kept = attend(qkv, key_ok)
    attn = sum_rows(context, proj_w, count)
    first, normed_a, inv_a = norm_forward(rows + attn, gain_a, shift_a)
    full_first = gather_rows(first.astype(jnp.bfloat16))
    pre = jnp.dot(full_first, in_w, preferred_element_type=jnp.float32)
    act = jax.nn.gelu(pre, approximate=False).astype(jnp.bfloat16)
    ffn = sum_rows(act, out_w, count)
    result, normed_f, inv_f = norm_forward(first + ffn, gain_f, shift_f)
    return (
        result,
        (full, att_kept, context, normed_a, inv_a, full_first, pre, act, normed_f, inv_f),
    )


def block_backward(grad_out, weights, key_ok, count, kept):
    qkv_w, proj_w, gain_a, shift_a, in_w, out_w, gain_f, shift_f = weights
    full, att_kept, context, normed_a, inv_a, full_first, pre, act, normed_f, inv_f = kept
    grad_second, grad_gain_f, grad_shift_f = norm_backward(grad_out, normed_f, inv_f, gain_f)
    full_grad_ffn = gather_grad(grad_second.astype(jnp.bfloat16))
    grad_act = contract_last(full_grad_ffn, out_w)
    grad_out_w = contract_rows(act, full_grad_ffn)
    grad_pre = (grad_act * gelu_slope(pre)).astype(jnp.bfloat16)
    grad_in_w = contract_rows(full_first, grad_pre)

    def ffn_term(start, size):
        return contract_last(grad_pre, in_w)

    grad_first = grad_second + sum_back(ffn_term, count)
    grad_resid, grad_gain_a, grad_shift_a = norm_backward(grad_first, normed_a, inv_a, gain_a)
    full_grad_attn = gather_grad(grad_resid.astype(jnp.bfloat16))
    grad_ctx = contract_last(full_grad_attn, proj_w).astype(jnp.bfloat16)
    grad_proj = contract_rows(context, full_grad_attn)
    grad_qkv = attend_back(grad_ctx, att_kept, key_ok)
    grad_qkv_w = jnp.einsum("rd,rcj->cdj", full, grad_qkv, preferred_element_type=jnp.float32)

    def attn_term(start, size):
        return jnp.einsum("rcj,cdj->rd", grad_qkv, qkv_w, preferred_element_type=jnp.float32)

    grad_rows = grad_resid + sum_back(attn_term, count)
    return (
        grad_rows,
        (grad_qkv_w, grad_proj, grad_in_w, grad_out_w),
        (grad_gain_a, grad_shift_a, grad_gain_f, grad_shift_f),
    )


def on_device(
    tokens,
    skip_tokens,
    cot_back,
    cot_head,
    one_span,
    lower_qkv,
    lower_proj,
    lower_gain_attn,
    lower_shift_attn,
    lower_w_in,
    lower_w_out,
    lower_gain_ffn,
    lower_shift_ffn,
    upper_qkv,
    upper_proj,
    upper_gain_attn,
    upper_shift_attn,
    upper_w_in,
    upper_w_out,
    upper_gain_ffn,
    upper_shift_ffn,
):
    count = tokens.shape[0]
    docs_local = one_span.shape[0]
    position = jnp.arange(2 * SPAN)
    key_ok = (position[None, :] < SPAN) | (one_span[:, None] == 0)
    row_index = lax.axis_index("tensor") * count + jnp.arange(count)
    doc_index = row_index // (2 * SPAN)
    doc_flag = jnp.sum(
        jnp.where(doc_index[:, None] == jnp.arange(docs_local)[None, :], one_span[None, :], 0),
        axis=1,
    )
    row_ok = (row_index // SPAN % 2 == 0) | (doc_flag == 0)
    valid = row_ok[:, None].astype(jnp.float32)
    is_cls = (row_index % SPAN == 0)[:, None]
    lower = (
        lower_qkv,
        lower_proj,
        lower_gain_attn,
        lower_shift_attn,
        lower_w_in,
        lower_w_out,
        lower_gain_ffn,
        lower_shift_ffn,
    )
    upper = (
        upper_qkv,
        upper_proj,
        upper_gain_attn,
        upper_shift_attn,
        upper_w_in,
        upper_w_out,
        upper_gain_ffn,
        upper_shift_ffn,
    )
    back, kept_lower = block_forward(tokens.astype(jnp.float32), lower, key_ok, count)
    head_in = jnp.where(is_cls, back, skip_tokens.astype(jnp.float32))
    head, kept_upper = block_forward(head_in, upper, key_ok, count)
    head_again, kept_upper = block_forward(head_in, upper, key_ok, count)
    grad_head_in, weights_upper, norms_upper = block_backward(
        cot_head.astype(jnp.float32) * valid, upper, key_ok, count, kept_upper
    )
    grad_skip = jnp.where(is_cls, 0.0, grad_head_in)
    grad_back = cot_back.astype(jnp.float32) * valid + jnp.where(is_cls, grad_head_in, 0.0)
    back_again, kept_lower = block_forward(tokens.astype(jnp.float32), lower, key_ok, count)
    grad_tokens, weights_lower, norms_lower = block_backward(
        grad_back, lower, key_ok, count, kept_lower
    )
    summed = lax.psum(
        (
            weights_lower[0],
            weights_lower[1],
            weights_lower[2],
            weights_lower[3],
            weights_upper[0],
            weights_upper[1],
            weights_upper[2],
            weights_upper[3],
        ),
        "dp",
    )
    weights_lower = summed[:4]
    weights_upper = summed[4:]
    norms = lax.psum(
        (
            norms_lower[0],
            norms_lower[1],
            norms_lower[2],
            norms_lower[3],
            norms_upper[0],
            norms_upper[1],
            norms_upper[2],
            norms_upper[3],
        ),
        ("dp", "tensor"),
    )
    return (
        (back * valid).astype(jnp.bfloat16),
        (head * valid).astype(jnp.bfloat16),
        grad_tokens,
        grad_skip,
        weights_lower[0],
        weights_lower[1],
        norms[0],
        norms[1],
        weights_lower[2],
        weights_lower[3],
        norms[2],
        norms[3],
        weights_upper[0],
        weights_upper[1],
        norms[4],
        norms[5],
        weights_upper[2],
        weights_upper[3],
        norms[6],
        norms[7],
    )


def solution(mesh):
    return jax.shard_map(
        on_device,
        mesh=mesh,
        in_specs=(
            P(("dp", "tensor"), None),
            P(("dp", "tensor"), None),
            P(("dp", "tensor"), None),
            P(("dp", "tensor"), None),
            P("dp"),
            P(None, None, "tensor"),
            P("tensor", None),
            P(),
            P(),
            P(None, "tensor"),
            P("tensor", None),
            P(),
            P(),
            P(None, None, "tensor"),
            P("tensor", None),
            P(),
            P(),
            P(None, "tensor"),
            P("tensor", None),
            P(),
            P(),
        ),
        out_specs=(
            P(("dp", "tensor"), None),
            P(("dp", "tensor"), None),
            P(("dp", "tensor"), None),
            P(("dp", "tensor"), None),
            P(None, None, "tensor"),
            P("tensor", None),
            P(),
            P(),
            P(None, "tensor"),
            P("tensor", None),
            P(),
            P(),
            P(None, None, "tensor"),
            P("tensor", None),
            P(),
            P(),
            P(None, "tensor"),
            P("tensor", None),
            P(),
            P(),
        ),
        check_vma=False,
    )
```

profile of v0, /device:TPU:1, one launch (start us, length us, event | category | flops | bytes accessed | tf_op | source)
XLA Modules:
  0.0 769.2 jit_solution(13849110559285241744)
XLA Ops:
  8.7 16.6 %all-gather.9.cloned.1.call-done = bf16[768,768]{1,0:T(8,128)(2,1)} async-done(((bf16[384,768]{1,0:T(8,128)(2,1)}), bf16[768,768]{1,0:T(8,128)(2,1)}) %all-gather.9.cloned.1.call-update) | async-done | bytes 1179664 | tf_op jit(solution)/shard_map/all_gather | solution.py:50
  50.5 12.8 %reduce-scatter.9.cloned.1.call-done = bf16[384,768]{1,0:T(8,128)(2,1)} async-done(((bf16[768,768]{1,0:T(8,128)(2,1)}), bf16[384,768]{1,0:T(8,128)(2,1)}) %reduce-scatter.9.cloned.1.call-update) | async-done | bytes 589840 | tf_op jit(solution)/shard_map/reduce_scatter | solution.py:62
  67.8 12.9 %all-gather.11.cloned.1.call-done = bf16[768,768]{1,0:T(8,128)(2,1)} async-done(((bf16[384,768]{1,0:T(8,128)(2,1)}), bf16[768,768]{1,0:T(8,128)(2,1)}) %all-gather.11.cloned.1.call-update) | async-done | bytes 1179664 | tf_op jit(solution)/shard_map/all_gather | solution.py:50
  80.7 14.4 %fusion.2 = (bf16[768,1536]{1,0:T(8,128)(2,1)S(1)}, f32[768,1536]{1,0:T(8,128)}) fusion(bf16[768,768]{1,0:T(8,128)(2,1)} %all-gather.11.cloned.1.call-done, bf16[768,1536]{1,0:T(8,128)(2,1)} %param.30), kind=kOutput, calls=%fused_computation.6 | convolution fusion | flops 1888616448 | bytes 10616832 | tf_op jit(solution)/shard_map/dot_general | solution.py:144
  100.1 12.3 %reduce-scatter.11.cloned.1.call-done = bf16[384,768]{1,0:T(8,128)(2,1)} async-done(((bf16[768,768]{1,0:T(8,128)(2,1)}), bf16[384,768]{1,0:T(8,128)(2,1)}) %reduce-scatter.11.cloned.1.call-update) | async-done | bytes 589840 | tf_op jit(solution)/shard_map/reduce_scatter | solution.py:62
  118.6 13.2 %all-gather.13.cloned.1.call-done = bf16[768,768]{1,0:T(8,128)(2,1)} async-done(((bf16[384,768]{1,0:T(8,128)(2,1)}), bf16[768,768]{1,0:T(8,128)(2,1)}) %all-gather.13.cloned.1.call-update) | async-done | bytes 1179664 | tf_op jit(solution)/shard_map/all_gather | solution.py:50
  163.4 11.5 %reduce-scatter.13.cloned.1.call-done = bf16[384,768]{1,0:T(8,128)(2,1)} async-done(((bf16[768,768]{1,0:T(8,128)(2,1)}), bf16[384,768]{1,0:T(8,128)(2,1)}) %reduce-scatter.13.cloned.1.call-update) | async-done | bytes 589840 | tf_op jit(solution)/shard_map/reduce_scatter | solution.py:62
  180.7 13.2 %all-gather.15.cloned.1.call-done = bf16[768,768]{1,0:T(8,128)(2,1)} async-done(((bf16[384,768]{1,0:T(8,128)(2,1)}), bf16[768,768]{1,0:T(8,128)(2,1)}) %all-gather.15.cloned.1.call-update) | async-done | bytes 1179664 | tf_op jit(solution)/shard_map/all_gather | solution.py:50
  193.9 13.7 %fusion.5 = (bf16[768,1536]{1,0:T(8,128)(2,1)S(1)}, f32[768,1536]{1,0:T(8,128)}) fusion(bf16[768,768]{1,0:T(8,128)(2,1)} %all-gather.15.cloned.1.call-done, bf16[768,1536]{1,0:T(8,128)(2,1)S(1)} %copy-done), kind=kOutput, calls=%fused_computation.9 | convolution fusion | flops 1888616448 | bytes 10616832 | tf_op jit(solution)/shard_map/dot_general | solution.py:144
  212.1 12.8 %reduce-scatter.15.cloned.1.call-done = bf16[384,768]{1,0:T(8,128)(2,1)} async-done(((bf16[768,768]{1,0:T(8,128)(2,1)}), bf16[384,768]{1,0:T(8,128)(2,1)}) %reduce-scatter.15.cloned.1.call-update) | async-done | bytes 589840 | tf_op jit(solution)/shard_map/reduce_scatter | solution.py:62
  232.0 13.4 %all-gather.17.cloned.1.call-done = bf16[768,768]{1,0:T(8,128)(2,1)} async-done(((bf16[384,768]{1,0:T(8,128)(2,1)}), bf16[768,768]{1,0:T(8,128)(2,1)}) %all-gather.17.cloned.1.call-update) | async-done | bytes 1179664 | tf_op jit(solution)/shard_map/all_gather | solution.py:54
  245.3 5.4 fusion.11
  255.2 12.8 %reduce-scatter.17.cloned.1.call-done = bf16[384,768]{1,0:T(8,128)(2,1)} async-done(((bf16[768,768]{1,0:T(8,128)(2,1)}), bf16[384,768]{1,0:T(8,128)(2,1)}) %reduce-scatter.17.cloned.1.call-update) | async-done | bytes 589840 | tf_op jit(solution)/shard_map/reduce_scatter | solution.py:71
  274.8 12.2 %all-gather.19.cloned.1.call-done = bf16[768,768]{1,0:T(8,128)(2,1)} async-done(((bf16[384,768]{1,0:T(8,128)(2,1)}), bf16[768,768]{1,0:T(8,128)(2,1)}) %all-gather.19.cloned.1.call-update) | async-done | bytes 1179664 | tf_op jit(solution)/shard_map/all_gather | solution.py:54
  319.0 12.8 %reduce-scatter.19.cloned.1.call-done = bf16[384,768]{1,0:T(8,128)(2,1)} async-done(((bf16[768,768]{1,0:T(8,128)(2,1)}), bf16[384,768]{1,0:T(8,128)(2,1)}) %reduce-scatter.19.cloned.1.call-update) | async-done | bytes 589840 | tf_op jit(solution)/shard_map/reduce_scatter | solution.py:71
  336.8 13.2 %all-gather.21.cloned.1.call-done = bf16[768,768]{1,0:T(8,128)(2,1)} async-done(((bf16[384,768]{1,0:T(8,128)(2,1)}), bf16[768,768]{1,0:T(8,128)(2,1)}) %all-gather.21.cloned.1.call-update) | async-done | bytes 1179664 | tf_op jit(solution)/shard_map/all_gather | solution.py:54
  350.0 5.5 fusion.17
  360.0 12.8 %reduce-scatter.21.cloned.1.call-done = bf16[384,768]{1,0:T(8,128)(2,1)} async-done(((bf16[768,768]{1,0:T(8,128)(2,1)}), bf16[384,768]{1,0:T(8,128)(2,1)}) %reduce-scatter.21.cloned.1.call-update) | async-done | bytes 589840 | tf_op jit(solution)/shard_map/reduce_scatter | solution.py:71
  377.1 6.4 fusion.109
  439.2 69.9 %all-reduce = (f32[768]{0:T(1024)}, f32[768]{0:T(1024)}, f32[768]{0:T(1024)}, f32[768]{0:T(1024)}, f32[768]{0:T(1024)}, /*index=5*/f32[768]{0:T(1024)}, f32[768]{0:T(1024)}, f32[768]{0:T(1024)}) all-reduce(f32[768]{0:T(1024)S(1)} %get-tuple-element.82, f32[768]{0:T(1024)S(1)} %copy-done.68, ...), channel_id=1, replica_groups=mesh['dp'=64,'tensor'=2] {'dp','tensor'}, use_global_device_ids=true, to_apply=%region_34.35 | all-reduce | flops 6144 | bytes 49152 | tf_op jit(solution)/shard_map/psum | solution.py:270
  511.3 223.8 %all-reduce.4.cloned.1.call-done = (f32[3,768,384]{1,2,0:T(8,128)}, f32[384,768]{1,0:T(8,128)}, f32[768,1536]{1,0:T(8,128)}, f32[1536,768]{1,0:T(8,128)}, f32[3,...) async-done(((f32[3,768,384]{1,2,0:T(8,128)}, f32[384,768]{1,0:T(8,128)}, f32[768,1536]{1,0:T(8,128)}, f32[1536,768]{1,0:T(8,128)}, ...) | async-done | bytes 28311568 | tf_op jit(solution)/shard_map/psum | solution.py:255
  735.1 5.2 copy.167
  740.3 5.3 copy.168
  746.6 5.5 copy.222
  (361 shorter events, 216.4 us)
Async XLA Ops:
  7.2 186.7 %copy-start = (bf16[768,1536]{1,0:T(8,128)(2,1)S(1)}, bf16[768,1536]{1,0:T(8,128)(2,1)}, u32[]{:S(2)}) copy-start(bf16[768,1536]{1,0:T(8,128)(2,1)} %param.38) | copy-start | bytes 7077892
  7.2 18.1 %all-gather.9.cloned.1.call-start = ((), (), s32[]{:S(2)}) async-start(), calls=%async_computation.8 | async-start | bytes 1769472 | tf_op jit(solution)/shard_map/all_gather | solution.py:50
  7.9 55.3 %reduce-scatter.9.cloned.1.call-start = ((), (), s32[]{:S(2)}) async-start(), calls=%async_computation.9 | async-start | bytes 1769472 | tf_op jit(solution)/shard_map/reduce_scatter | solution.py:62
  8.7 34.0 %copy-start.71 = (pred[3,256]{1,0:T(4,128)(4,1)}, pred[3,256]{1,0:T(4,128)(4,1)S(1)}, u32[]{:S(2)}) copy-start(pred[3,256]{1,0:T(4,128)(4,1)S(1)} %broadcast_or_fusion) | copy-start | bytes 2308
  50.4 30.2 %all-gather.11.cloned.1.call-start = ((), (), s32[]{:S(2)}) async-start(), calls=%async_computation.10 | async-start | bytes 1769472 | tf_op jit(solution)/shard_map/all_gather | solution.py:50
  67.2 45.1 %reduce-scatter.11.cloned.1.call-start = ((), (), s32[]{:S(2)}) async-start(), calls=%async_computation.11 | async-start | bytes 1769472 | tf_op jit(solution)/shard_map/reduce_scatter | solution.py:62
  80.7 15.8 %copy-start.75 = (bf16[1536,768]{1,0:T(8,128)(2,1)S(1)}, bf16[1536,768]{1,0:T(8,128)(2,1)}, u32[]{:S(2)}) copy-start(bf16[1536,768]{1,0:T(8,128)(2,1)} %param.31) | copy-start | bytes 7077892
  99.5 32.3 %all-gather.13.cloned.1.call-start = ((), (), s32[]{:S(2)}) async-start(), calls=%async_computation.12 | async-start | bytes 1769472 | tf_op jit(solution)/shard_map/all_gather | solution.py:50
  118.4 56.5 %reduce-scatter.13.cloned.1.call-start = ((), (), s32[]{:S(2)}) async-start(), calls=%async_computation.13 | async-start | bytes 1769472 | tf_op jit(solution)/shard_map/reduce_scatter | solution.py:62
  162.0 31.8 %all-gather.15.cloned.1.call-start = ((), (), s32[]{:S(2)}) async-start(), calls=%async_computation.14 | async-start | bytes 1769472 | tf_op jit(solution)/shard_map/all_gather | solution.py:50
  180.4 44.5 %reduce-scatter.15.cloned.1.call-start = ((), (), s32[]{:S(2)}) async-start(), calls=%async_computation.15 | async-start | bytes 1769472 | tf_op jit(solution)/shard_map/reduce_scatter | solution.py:62
  212.0 33.3 %all-gather.17.cloned.1.call-start = ((), (), s32[]{:S(2)}) async-start(), calls=%async_computation.16 | async-start | bytes 1769472 | tf_op jit(solution)/shard_map/all_gather | solution.py:54
  231.9 36.1 %reduce-scatter.17.cloned.1.call-start = ((), (), s32[]{:S(2)}) async-start(), calls=%async_computation.17 | async-start | bytes 1769472 | tf_op jit(solution)/shard_map/reduce_scatter | solution.py:71
  255.2 16.0 %copy-start.6 = (f32[384,768]{1,0:T(8,128)S(1)}, f32[384,768]{1,0:T(8,128)}, u32[]{:S(2)}) copy-start(f32[384,768]{1,0:T(8,128)} %copy-done.5) | copy-start | bytes 3538948
  255.2 16.0 %copy-start.9 = (f32[384,768]{1,0:T(8,128)S(1)}, f32[384,768]{1,0:T(8,128)}, u32[]{:S(2)}) copy-start(f32[384,768]{1,0:T(8,128)} %get-tuple-element.120) | copy-start | bytes 3538948
  255.2 31.8 %all-gather.19.cloned.1.call-start = ((), (), s32[]{:S(2)}) async-start(), calls=%async_computation.18 | async-start | bytes 1769472 | tf_op jit(solution)/shard_map/all_gather | solution.py:54
  273.5 58.3 %reduce-scatter.19.cloned.1.call-start = ((), (), s32[]{:S(2)}) async-start(), calls=%async_computation.19 | async-start | bytes 1769472 | tf_op jit(solution)/shard_map/reduce_scatter | solution.py:71
  274.7 20.4 %copy-start.45 = (f32[3,6,256]{2,1,0:T(8,128)}, f32[3,6,256]{2,1,0:T(8,128)S(1)}, u32[]{:S(2)}) copy-start(f32[3,6,256]{2,1,0:T(8,128)S(1)} %log_add_fusion.1) | copy-start | bytes 55300
  319.0 31.0 %all-gather.21.cloned.1.call-start = ((), (), s32[]{:S(2)}) async-start(), calls=%async_computation.20 | async-start | bytes 1769472 | tf_op jit(solution)/shard_map/all_gather | solution.py:54
  336.6 36.3 %reduce-scatter.21.cloned.1.call-start = ((), (), s32[]{:S(2)}) async-start(), calls=%async_computation.21 | async-start | bytes 1769472 | tf_op jit(solution)/shard_map/reduce_scatter | solution.py:71
  360.0 30.5 %all-gather.23.cloned.1.call-start = ((), (), s32[]{:S(2)}) async-start(), calls=%async_computation.22 | async-start | bytes 1769472 | tf_op jit(solution)/shard_map/all_gather | solution.py:54
  377.0 132.1 %reduce-scatter.23.cloned.1.call-start = ((), (), s32[]{:S(2)}) async-start(), calls=%async_computation.23 | async-start | bytes 1769472 | tf_op jit(solution)/shard_map/reduce_scatter | solution.py:71
  417.3 317.9 %all-reduce.4.cloned.1.call-start = ((), (), s32[]{:S(2)}) async-start(), calls=%async_computation.24 | async-start | bytes 56623104 | tf_op jit(solution)/shard_map/psum | solution.py:255
  438.5 70.7 %copy-start.17 = (f32[384,768]{1,0:T(8,128)S(1)}, f32[384,768]{1,0:T(8,128)}, u32[]{:S(2)}) copy-start(f32[384,768]{1,0:T(8,128)} %get-tuple-element.113) | copy-start | bytes 3538948
  (91 other events, 389.4 us)
Sparse Core Ops, SparseCore 0:
  9.7 15.5 all-gather.8
  50.5 12.6 reduce-scatter.8
  67.3 13.2 all-gather.10
  99.6 12.6 reduce-scatter.10
  118.5 13.2 all-gather.12
  162.1 12.7 reduce-scatter.12
  180.5 13.2 all-gather.14
  212.2 12.6 reduce-scatter.14
  232.0 13.2 all-gather.16
  255.3 12.6 reduce-scatter.16
  273.6 13.2 all-gather.18
  319.1 12.6 reduce-scatter.18
  336.7 13.2 all-gather.20
  360.1 12.6 reduce-scatter.20
  377.2 13.2 all-gather.22
  417.4 12.6 reduce-scatter.22
  438.6 296.4 all-reduce.3
where the time goes:
time: 777 us; the launch traced here: 769 us
  waiting for transfers between devices  410 us (53%)
  matrix products  128 us (16%)
  local copies, waits for them, and re-layouts  98.2 us (13%)
  blocking collectives  69.9 us (9%)
  other arithmetic  45.2 us (6%)
  between operations  15.4 us (2%)
    psum x1, waiting for transfers between devices, on_device(): lax.psum((weights_lower[0], weights_lower[1], weights_lower[2], weights_l...  224 us
    psum x1, blocking collectives, on_device(): lax.psum((norms_lower[0], norms_lower[1], norms_lower[2], norms_lower[3],...  69.9 us
    all_gather x4, waiting for transfers between devices, gather_rows(): return lax.all_gather(rows_low, 'tensor', axis=0, tiled=True)  55.8 us
    reduce_scatter x4, waiting for transfers between devices, sum_rows(): lax.psum_scatter(term(jnp.int32(0), count * lax.axis_size('tensor')).asty...  49.3 us
    unnamed x210, local copies, waits for them, and re-layouts  46 us
    all_gather x4, waiting for transfers between devices, gather_grad(): return lax.all_gather(rows_low, 'tensor', axis=0, tiled=True)  41.5 us
    reduce_scatter x4, waiting for transfers between devices, sum_back(): lax.psum_scatter(term(jnp.int32(0), count * lax.axis_size('tensor')).asty...  38.4 us
    dot_general x2, matrix products, block_forward(): pre = jnp.dot(full_first, in_w, preferred_element_type=jnp.float32)  28.1 us
  transfers between devices with their start and end apart: 17, of which 16 were waited for; matrix products, arithmetic and copies ran while one was open for 5% of the time, Pallas kernels for 0%

commit v1 on v0

--- a/solution.py
+++ b/solution.py
@@ -47,7 +47,9 @@
 
 
 def gather_rows(rows_low):
-    return lax.all_gather(rows_low, "tensor", axis=0, tiled=True)
+    return jnp.concatenate(
+        lax.all_to_all(jnp.stack([rows_low] * lax.axis_size("tensor")), "tensor", 0, 0), axis=0
+    )
 
 
 def gather_grad(rows_low):

time: 777 us -> 737 us (0.949)
  waiting for transfers between devices: 410 us -> 357 us
  blocking collectives: 69.9 us -> 84.5 us
    all_gather x4 -> x0, waiting for transfers between devices: 55.8 us -> none  [gather_rows(): return lax.all_gather(rows_low, 'tensor', axis=0, tiled=True)]
    all_to_all x0 -> x3, blocking collectives: none -> 14.5 us  [gather_rows(): lax.all_to_all(jnp.stack([rows_low] * lax.axis_size('tensor')), 'tensor',...]
    unnamed x210 -> x228, local copies, waits for them, and re-layouts: 46 us -> 44.8 us
  transfers between devices with their start and end apart: 17 -> 14, of which waited for: 16 -> 13; matrix products, arithmetic and copies ran while one was open for 5% -> 5% of each run, Pallas kernels for 0% -> 0%
where the time goes in v1:
time: 737 us; the launch traced here: 729 us
  waiting for transfers between devices  357 us (48%)
  matrix products  125 us (17%)
  local copies, waits for them, and re-layouts  97.3 us (13%)
  blocking collectives  84.5 us (11%)
  other arithmetic  43.4 us (6%)
  between operations  15.2 us (2%)
    psum x1, waiting for transfers between devices, on_device(): lax.psum((weights_lower[0], weights_lower[1], weights_lower[2], weights_l...  224 us
    psum x1, blocking collectives, on_device(): lax.psum((norms_lower[0], norms_lower[1], norms_lower[2], norms_lower[3],...  70 us
    reduce_scatter x4, waiting for transfers between devices, sum_rows(): lax.psum_scatter(term(jnp.int32(0), count * lax.axis_size('tensor')).asty...  51.4 us
    unnamed x228, local copies, waits for them, and re-layouts  44.8 us
    all_gather x4, waiting for transfers between devices, gather_grad(): return lax.all_gather(rows_low, 'tensor', axis=0, tiled=True)  41.1 us
    reduce_scatter x4, waiting for transfers between devices, sum_back(): lax.psum_scatter(term(jnp.int32(0), count * lax.axis_size('tensor')).asty...  38.4 us
    dot_general x2, matrix products, block_forward(): pre = jnp.dot(full_first, in_w, preferred_element_type=jnp.float32)  25.4 us
    dot_general x6, matrix products, contract_rows(): lax.dot_general(left, right, (((0,), (0,)), ((), ())), preferred_element_...  23.6 us
  transfers between devices with their start and end apart: 14, of which 13 were waited for; matrix products, arithmetic and copies ran while one was open for 5% of the time, Pallas kernels for 0%

profile of v1, /device:TPU:1, one launch (start us, length us, event | category | flops | bytes accessed | tf_op | source)
XLA Modules:
  0.0 728.8 jit_solution(6761575692141350556)
XLA Ops:
  9.7 5.9 all-to-all-start
  42.9 14.0 %reduce-scatter.9.cloned.1.call-done = bf16[384,768]{1,0:T(8,128)(2,1)} async-done(((bf16[768,768]{1,0:T(8,128)(2,1)}), bf16[384,768]{1,0:T(8,128)(2,1)}) %reduce-scatter.9.cloned.1.call-update) | async-done | bytes 589840 | tf_op jit(solution)/shard_map/reduce_scatter | solution.py:64
  60.2 4.9 all_to_all.24
  65.1 12.7 %fusion.2 = (bf16[768,1536]{1,0:T(8,128)(2,1)S(1)}, f32[768,1536]{1,0:T(8,128)}) fusion(bf16[768,768]{1,0:T(8,128)(2,1)S(1)} %bitcast.140, bf16[768,1536]{1,0:T(8,128)(2,1)S(1)} %copy-done.83), kind=kOutput, calls=%fused_computation.6 | convolution fusion | flops 1888616448 | bytes 10616832 | tf_op jit(solution)/shard_map/dot_general | solution.py:146
  82.8 12.5 %reduce-scatter.11.cloned.1.call-done = bf16[384,768]{1,0:T(8,128)(2,1)} async-done(((bf16[768,768]{1,0:T(8,128)(2,1)}), bf16[384,768]{1,0:T(8,128)(2,1)}) %reduce-scatter.11.cloned.1.call-update) | async-done | bytes 589840 | tf_op jit(solution)/shard_map/reduce_scatter | solution.py:64
  99.5 5.1 all_to_all.25
  134.3 11.7 %reduce-scatter.13.cloned.1.call-done = bf16[384,768]{1,0:T(8,128)(2,1)} async-done(((bf16[768,768]{1,0:T(8,128)(2,1)}), bf16[384,768]{1,0:T(8,128)(2,1)}) %reduce-scatter.13.cloned.1.call-update) | async-done | bytes 589840 | tf_op jit(solution)/shard_map/reduce_scatter | solution.py:64
  154.8 12.7 %fusion.5 = (bf16[768,1536]{1,0:T(8,128)(2,1)S(1)}, f32[768,1536]{1,0:T(8,128)}) fusion(bf16[768,768]{1,0:T(8,128)(2,1)S(1)} %bitcast.142, bf16[768,1536]{1,0:T(8,128)(2,1)S(1)} %copy-done), kind=kOutput, calls=%fused_computation.9 | convolution fusion | flops 1888616448 | bytes 10616832 | tf_op jit(solution)/shard_map/dot_general | solution.py:146
  172.0 13.1 %reduce-scatter.15.cloned.1.call-done = bf16[384,768]{1,0:T(8,128)(2,1)} async-done(((bf16[768,768]{1,0:T(8,128)(2,1)}), bf16[384,768]{1,0:T(8,128)(2,1)}) %reduce-scatter.15.cloned.1.call-update) | async-done | bytes 589840 | tf_op jit(solution)/shard_map/reduce_scatter | solution.py:64
  191.5 13.4 %all-gather.5.cloned.1.call-done = bf16[768,768]{1,0:T(8,128)(2,1)} async-done(((bf16[384,768]{1,0:T(8,128)(2,1)}), bf16[768,768]{1,0:T(8,128)(2,1)}) %all-gather.5.cloned.1.call-update) | async-done | bytes 1179664 | tf_op jit(solution)/shard_map/all_gather | solution.py:56
  204.8 5.4 fusion.11
  214.7 12.8 %reduce-scatter.17.cloned.1.call-done = bf16[384,768]{1,0:T(8,128)(2,1)} async-done(((bf16[768,768]{1,0:T(8,128)(2,1)}), bf16[384,768]{1,0:T(8,128)(2,1)}) %reduce-scatter.17.cloned.1.call-update) | async-done | bytes 589840 | tf_op jit(solution)/shard_map/reduce_scatter | solution.py:73
  233.7 12.4 %all-gather.7.cloned.1.call-done = bf16[768,768]{1,0:T(8,128)(2,1)} async-done(((bf16[384,768]{1,0:T(8,128)(2,1)}), bf16[768,768]{1,0:T(8,128)(2,1)}) %all-gather.7.cloned.1.call-update) | async-done | bytes 1179664 | tf_op jit(solution)/shard_map/all_gather | solution.py:56
  278.1 12.8 %reduce-scatter.19.cloned.1.call-done = bf16[384,768]{1,0:T(8,128)(2,1)} async-done(((bf16[768,768]{1,0:T(8,128)(2,1)}), bf16[384,768]{1,0:T(8,128)(2,1)}) %reduce-scatter.19.cloned.1.call-update) | async-done | bytes 589840 | tf_op jit(solution)/shard_map/reduce_scatter | solution.py:73
  295.9 13.1 %all-gather.9.cloned.1.call-done = bf16[768,768]{1,0:T(8,128)(2,1)} async-done(((bf16[384,768]{1,0:T(8,128)(2,1)}), bf16[768,768]{1,0:T(8,128)(2,1)}) %all-gather.9.cloned.1.call-update) | async-done | bytes 1179664 | tf_op jit(solution)/shard_map/all_gather | solution.py:56
  309.1 5.5 fusion.17
  319.1 12.8 %reduce-scatter.21.cloned.1.call-done = bf16[384,768]{1,0:T(8,128)(2,1)} async-done(((bf16[768,768]{1,0:T(8,128)(2,1)}), bf16[384,768]{1,0:T(8,128)(2,1)}) %reduce-scatter.21.cloned.1.call-update) | async-done | bytes 589840 | tf_op jit(solution)/shard_map/reduce_scatter | solution.py:73
  337.0 6.0 fusion.107
  393.6 4.7 convolution_bitcast_fusion.1
  399.1 70.0 %all-reduce = (f32[768]{0:T(1024)}, f32[768]{0:T(1024)}, f32[768]{0:T(1024)}, f32[768]{0:T(1024)}, f32[768]{0:T(1024)}, /*index=5*/f32[768]{0:T(1024)}, f32[768]{0:T(1024)}, f32[768]{0:T(1024)}) all-reduce(f32[768]{0:T(1024)S(1)} %get-tuple-element.82, f32[768]{0:T(1024)S(1)} %copy-done.72, ...), channel_id=1, replica_groups=mesh['dp'=64,'tensor'=2] {'dp','tensor'}, use_global_device_ids=true, to_apply=%region_34.35 | all-reduce | flops 6144 | bytes 49152 | tf_op jit(solution)/shard_map/psum | solution.py:272
  471.3 223.7 %all-reduce.4.cloned.1.call-done = (f32[3,768,384]{1,2,0:T(8,128)}, f32[384,768]{1,0:T(8,128)}, f32[768,1536]{1,0:T(8,128)}, f32[1536,768]{1,0:T(8,128)}, f32[3,...) async-done(((f32[3,768,384]{1,2,0:T(8,128)}, f32[384,768]{1,0:T(8,128)}, f32[768,1536]{1,0:T(8,128)}, f32[1536,768]{1,0:T(8,128)}, ...) | async-done | bytes 28311568 | tf_op jit(solution)/shard_map/psum | solution.py:257
  695.0 5.2 copy.167
  700.1 5.3 copy.168
  706.4 5.5 copy.222
  (376 shorter events, 212.4 us)
Async XLA Ops:
  7.2 147.6 %copy-start = (bf16[768,1536]{1,0:T(8,128)(2,1)S(1)}, bf16[768,1536]{1,0:T(8,128)(2,1)}, u32[]{:S(2)}) copy-start(bf16[768,1536]{1,0:T(8,128)(2,1)} %param.38) | copy-start | bytes 7077892
  9.7 7.9 %all-to-all-start = ((bf16[2,384,768]{2,1,0:T(8,128)(2,1)}), bf16[2,384,768]{2,1,0:T(8,128)(2,1)}, u32[]{:S(2)}, u32[]{:S(2)}) async-start(bf16[2,384,768]{2,1,0:T(8,128)(2,1)} %pad_maximum_fusion), calls=%async_computation | async-start | bytes 2359296 | tf_op jit(solution)/shard_map/all_to_all | solution.py:51
  15.6 41.3 %reduce-scatter.9.cloned.1.call-start = ((), (), s32[]{:S(2)}) async-start(), calls=%async_computation.12 | async-start | bytes 1769472 | tf_op jit(solution)/shard_map/reduce_scatter | solution.py:64
  41.0 15.9 %copy-start.4 = (bf16[384,768]{1,0:T(8,128)(2,1)S(1)}, bf16[384,768]{1,0:T(8,128)(2,1)}, u32[]{:S(2)}) copy-start(bf16[384,768]{1,0:T(8,128)(2,1)} %param.21) | copy-start | bytes 1769476
  42.8 16.9 %copy-start.54 = (f32[768]{0:T(1024)S(1)}, f32[768]{0:T(1024)}, u32[]{:S(2)}) copy-start(f32[768]{0:T(1024)} %param.28) | copy-start | bytes 9220
  42.8 16.9 %copy-start.57 = (f32[768]{0:T(1024)S(1)}, f32[768]{0:T(1024)}, u32[]{:S(2)}) copy-start(f32[768]{0:T(1024)} %param.29) | copy-start | bytes 9220
  42.9 52.5 %reduce-scatter.11.cloned.1.call-start = ((), (), s32[]{:S(2)}) async-start(), calls=%async_computation.13 | async-start | bytes 1769472 | tf_op jit(solution)/shard_map/reduce_scatter | solution.py:64
  82.2 63.8 %reduce-scatter.13.cloned.1.call-start = ((), (), s32[]{:S(2)}) async-start(), calls=%async_computation.14 | async-start | bytes 1769472 | tf_op jit(solution)/shard_map/reduce_scatter | solution.py:64
  131.0 15.0 %copy-start.60 = (f32[768]{0:T(1024)S(1)}, f32[768]{0:T(1024)}, u32[]{:S(2)}) copy-start(f32[768]{0:T(1024)} %param.32) | copy-start | bytes 9220
  132.9 52.2 %reduce-scatter.15.cloned.1.call-start = ((), (), s32[]{:S(2)}) async-start(), calls=%async_computation.15 | async-start | bytes 1769472 | tf_op jit(solution)/shard_map/reduce_scatter | solution.py:64
  171.9 32.9 %all-gather.5.cloned.1.call-start = ((), (), s32[]{:S(2)}) async-start(), calls=%async_computation.16 | async-start | bytes 1769472 | tf_op jit(solution)/shard_map/all_gather | solution.py:56
  191.4 36.1 %reduce-scatter.17.cloned.1.call-start = ((), (), s32[]{:S(2)}) async-start(), calls=%async_computation.17 | async-start | bytes 1769472 | tf_op jit(solution)/shard_map/reduce_scatter | solution.py:73
  214.7 15.6 %copy-start.9 = (f32[384,768]{1,0:T(8,128)S(1)}, f32[384,768]{1,0:T(8,128)}, u32[]{:S(2)}) copy-start(f32[384,768]{1,0:T(8,128)} %get-tuple-element.120) | copy-start | bytes 3538948
  214.7 31.4 %all-gather.7.cloned.1.call-start = ((), (), s32[]{:S(2)}) async-start(), calls=%async_computation.18 | async-start | bytes 1769472 | tf_op jit(solution)/shard_map/all_gather | solution.py:56
  232.6 58.3 %reduce-scatter.19.cloned.1.call-start = ((), (), s32[]{:S(2)}) async-start(), calls=%async_computation.19 | async-start | bytes 1769472 | tf_op jit(solution)/shard_map/reduce_scatter | solution.py:73
  233.6 20.5 %copy-start.47 = (f32[3,6,256]{2,1,0:T(8,128)}, f32[3,6,256]{2,1,0:T(8,128)S(1)}, u32[]{:S(2)}) copy-start(f32[3,6,256]{2,1,0:T(8,128)S(1)} %log_add_fusion.1) | copy-start | bytes 55300
  275.3 15.6 %copy-start.22 = (f32[384,768]{1,0:T(8,128)S(1)}, f32[384,768]{1,0:T(8,128)}, u32[]{:S(2)}) copy-start(f32[384,768]{1,0:T(8,128)} %get-tuple-element.118) | copy-start | bytes 3538948
  275.3 15.6 %copy-start.61 = (f32[768]{0:T(1024)S(1)}, f32[768]{0:T(1024)}, u32[]{:S(2)}) copy-start(f32[768]{0:T(1024)} %param.32) | copy-start | bytes 9220
  278.1 31.0 %all-gather.9.cloned.1.call-start = ((), (), s32[]{:S(2)}) async-start(), calls=%async_computation.20 | async-start | bytes 1769472 | tf_op jit(solution)/shard_map/all_gather | solution.py:56
  295.6 36.3 %reduce-scatter.21.cloned.1.call-start = ((), (), s32[]{:S(2)}) async-start(), calls=%async_computation.21 | async-start | bytes 1769472 | tf_op jit(solution)/shard_map/reduce_scatter | solution.py:73
  319.1 30.5 %all-gather.11.cloned.1.call-start = ((), (), s32[]{:S(2)}) async-start(), calls=%async_computation.22 | async-start | bytes 1769472 | tf_op jit(solution)/shard_map/all_gather | solution.py:56
  336.1 132.9 %reduce-scatter.23.cloned.1.call-start = ((), (), s32[]{:S(2)}) async-start(), calls=%async_computation.23 | async-start | bytes 1769472 | tf_op jit(solution)/shard_map/reduce_scatter | solution.py:73
  376.6 318.4 %all-reduce.4.cloned.1.call-start = ((), (), s32[]{:S(2)}) async-start(), calls=%async_computation.24 | async-start | bytes 56623104 | tf_op jit(solution)/shard_map/psum | solution.py:257
  398.3 70.7 %copy-start.21 = (f32[384,768]{1,0:T(8,128)S(1)}, f32[384,768]{1,0:T(8,128)}, u32[]{:S(2)}) copy-start(f32[384,768]{1,0:T(8,128)} %get-tuple-element.113) | copy-start | bytes 3538948
  (97 other events, 364.1 us)
Sparse Core Ops, SparseCore 0:
  43.0 13.9 reduce-scatter.8
  82.4 12.9 reduce-scatter.10
  133.0 12.9 reduce-scatter.12
  172.0 12.9 reduce-scatter.14
  191.5 13.2 all-gather.4
  214.8 12.6 reduce-scatter.16
  232.7 13.2 all-gather.6
  278.2 12.6 reduce-scatter.18
  295.8 13.2 all-gather.8
  319.2 12.6 reduce-scatter.20
  336.2 13.2 all-gather.10
  376.7 12.6 reduce-scatter.22
  398.5 296.4 all-reduce.3
